TPU v7x, 512 devices: a whole 4x4x16 slice. The times are simulated.
512 devices in a mesh: line: 32 (over y, x, core), bus: 16 (over z).
Axes of the slice: x: 4, y: 4, z: 16, core: 2. Of those that a mesh axis runs over, the one named last changes fastest.
Arguments:
- ptdf: bfloat16 [8192, 100352], P('line', 'bus')
- base_injection: float32 [100352], P('bus'), may hold values from -6 to 6
- injection_gain: float32 [100352], P('bus'), may hold values from 0.3 to 3
- factor_of_bus: int32 [100352], P('bus'), may hold values from 0 to 511
- line_rating: int32 [8192], P('line'), may hold values from 60 to 300
- directions: int32 [30, 512], replicated, may hold values from 1 to 1073741823, as said below
- shifts: int32 [8, 512], replicated, may hold values from 0 to 1073741823
- chol_factor: float32 [512, 512], replicated
- proposal_mean: float32 [512], replicated, may hold values from -0.3 to 0.3
Outputs:
- flows: float32 [1024, 8192], P('bus', 'line')
- overload: float32 [1024], P('bus')
- weight: float32 [1024], P('bus')
- new_mean: float32 [512], replicated
Inputs may be any that keep to these rules, and one draw needn't show every extreme that they name: directions[b, f] lies in [2^(29 - b), 2^(30 - b)), as Sobol direction numbers do.
All inputs are finite; a program needn't handle non-finite values.
Results may differ from a plain program's by a relative error of at most 0.0029.
Values sent between devices are 32-bit elements; how exact they have to be, the bound alone decides.
A program may use at most 64 MiB of HBM per device.

v0:
```python
import math
import jax
import jax.numpy as jnp
from jax import lax
from jax.sharding import PartitionSpec as P

POINTS = 128
SHARP = 8.0
HIGH = lax.Precision.HIGHEST


def normals(directions, shifts, start_row, row_count):
    scenario = start_row + jnp.arange(row_count, dtype=jnp.int32)
    sobol_point = scenario % POINTS
    shift_index = scenario // POINTS
    digits = jnp.zeros((row_count, directions.shape[1]), jnp.int32)
    for bit_index in range(max(1, (POINTS - 1).bit_length())):
        picked = sobol_point >> bit_index & 1
        digits = digits ^ picked[:, None] * directions[bit_index][None, :]
    chosen = (shift_index[:, None] == jnp.arange(shifts.shape[0], dtype=jnp.int32)[None, :]).astype(
        jnp.int32
    )
    offset = jnp.sum(chosen[:, :, None] * shifts[None, :, :], axis=1)
    digits = digits ^ offset
    uniform = (2 * (digits >> 7) + 1).astype(jnp.float32) / 16777216.0
    return math.sqrt(2.0) * lax.erf_inv(2.0 * uniform - 1.0)


def per_device(
    ptdf,
    base_injection,
    injection_gain,
    factor_of_bus,
    line_rating,
    directions,
    shifts,
    chol_factor,
    proposal_mean,
):
    bus_devices = lax.axis_size("bus")
    lines_total = ptdf.shape[0] * lax.axis_size("line")
    scenarios = POINTS * shifts.shape[0]
    block_rows = scenarios // bus_devices
    own_start = lax.axis_index("bus") * block_rows
    factors = lax.dot_general(
        normals(directions, shifts, 0, scenarios) + proposal_mean[None, :],
        chol_factor,
        (((1,), (1,)), ((), ())),
        precision=HIGH,
        preferred_element_type=jnp.float32,
    )
    rating = line_rating.astype(jnp.float32) * 0.01
    block_size = min(block_rows * lax.axis_size("bus"), 128)

    def one_block(index):
        rows = lax.dynamic_slice_in_dim(factors, index * block_size, block_size, 0)
        picked = jnp.take(rows, factor_of_bus, axis=1)
        injections = (base_injection[None, :] + injection_gain[None, :] * picked).astype(
            jnp.bfloat16
        )
        return lax.dot_general(
            injections, ptdf, (((1,), (1,)), ((), ())), preferred_element_type=jnp.float32
        )

    pieces = lax.map(
        one_block, jnp.arange(block_rows * lax.axis_size("bus") // block_size, dtype=jnp.int32)
    )
    flows = lax.psum_scatter(
        pieces.reshape(block_rows * lax.axis_size("bus"), ptdf.shape[0]),
        "bus",
        scatter_dimension=0,
        tiled=True,
    )
    own_normals = normals(directions, shifts, own_start, block_rows)
    likelihood = jnp.exp(
        -jnp.dot(own_normals, proposal_mean, precision=HIGH, preferred_element_type=jnp.float32)
    )
    share = (
        jnp.sum(jax.nn.softplus(SHARP * (jnp.abs(flows) / rating[None, :] - 1.0)), axis=1)
        / SHARP
        / lines_total
    )
    overload = lax.psum(share, "line")
    emphasis = likelihood * overload
    moved_part = jnp.dot(emphasis, own_normals, precision=HIGH, preferred_element_type=jnp.float32)
    moved, total = lax.psum((moved_part, jnp.sum(emphasis)), "bus")
    weight = scenarios * likelihood * overload / total
    new_mean = proposal_mean + moved / total
    return (flows, overload, weight, new_mean)


def solution(mesh):
    return jax.shard_map(
        per_device,
        mesh=mesh,
        in_specs=(P("line", "bus"), P("bus"), P("bus"), P("bus"), P("line"), P(), P(), P(), P()),
        out_specs=(P("bus", "line"), P("bus"), P("bus"), P()),
        check_vma=False,
    )
```

profile of v0, /device:TPU:32, one launch (start us, length us, event | category | flops | bytes accessed | tf_op | source)
XLA Modules:
  0.0 390.9 jit_solution(3735118935437047624)
XLA Ops:
  7.3 0.2 fusion.115
  7.5 1.0 fusion.158
  8.5 7.0 %multiply_reduce_fusion = s32[1024,512]{1,0:T(8,128)S(1)} fusion(s32[8,512]{1,0:T(8,128)} %param.17, s32[1024,8]{1,0:T(8,128)S(1)} %fusion.115), kind=kLoop, calls=%fused_computation.16 | loop fusion | flops 7864320 | bytes 2146304 | tf_op jit(solution)/shard_map/reduce_sum | solution.py:23
  15.6 9.1 %fusion.11 = f32[1024,512]{0,1:T(8,128)S(1)} fusion(f32[512,512]{1,0:T(8,128)S(1)} %copy-done, s32[1024,512]{1,0:T(8,128)S(1)} %multiply_reduce_fusion, f32[512]{0:T(512)S(1)} %copy-done.3, s32[512]{0:T(512)S(1)} %bitcast.46, s32[1024]{0:T(1024)S(1)} %get-tuple-element.98, s32[512]{0:T(512)S(1)} %bitcast.48, s32[1024]{0:T(1024)S(1)} %get-tuple-element.99, ...), kind=kOutput, calls=%fused_computation.20 | convolution fusion | flops 3252158464 | bytes 5287936 | tf_op jit(solution)/shard_map/dot_general | solution.py:45
  24.7 189.2 %while.10 = (s32[]{:T(128)}, f32[8,128,256]{2,1,0:T(8,128)}, f32[6272]{0:T(1024)S(1)}, f32[6272]{0:T(1024)}, s32[6272]{0:T(1024)S(1)}, /*index=5*/s32[8]{0:T(128...) while((s32[]{:T(128)}, f32[8,128,256]{2,1,0:T(8,128)}, ...), condition=%wide.region_2.3_spmd, body=%wide.region_1.2_spmd.sunk | while | flops 414316672 | bytes 13721023 | solution.py:65
  24.9 0.6 dynamic_slice.11
  26.2 0.1 fusion.168
  26.3 12.6 %gather_fusion = f32[6272,128]{1,0:T(8,128)} fusion(f32[128,512]{0,1:T(8,128)S(1)} %constant_dynamic-slice_fusion.2, s32[7168]{0:T(1024)S(1)} %pad_clamp_fusion.2), kind=kCustom, calls=%fused_computation.clone.1 | custom fusion | bytes 6447616 | tf_op jit(solution)/shard_map/while/body/eval_jaxpr/jit(_take)/gather | solution.py:57
  38.9 9.6 %fusion.169 = f32[8,128,256]{2,1,0:T(8,128)} fusion(f32[8,128,256]{2,1,0:T(8,128)} %get-tuple-element.172, s32[]{:T(128)S(6)} %copy.20, bf16[256,6272]{1,0:T(8,128)(2,1)} %get-tuple-element.190, f32[6272,128]{1,0:T(8,128)} %gather_fusion, f32[6272]{0:T(1024)S(1)} %get-tuple-element.185, f32[6272]{0:T(1024)} %get-tuple-element.186, ...), kind=kOutput, calls=%fused_computation.8.clone.1 | convolution fusion | flops 414253056 | bytes 6613636 | tf_op jit(solution)/shard_map/while/body/eval_jaxpr/dot_general | solution.py:61
  48.5 0.6 dynamic_slice.11
  49.8 0.1 fusion.168
  49.9 12.6 %gather_fusion = f32[6272,128]{1,0:T(8,128)} fusion(f32[128,512]{0,1:T(8,128)S(1)} %constant_dynamic-slice_fusion.2, s32[7168]{0:T(1024)S(1)} %pad_clamp_fusion.2), kind=kCustom, calls=%fused_computation.clone.1 | custom fusion | bytes 6447616 | tf_op jit(solution)/shard_map/while/body/eval_jaxpr/jit(_take)/gather | solution.py:57
  62.5 9.6 %fusion.169 = f32[8,128,256]{2,1,0:T(8,128)} fusion(f32[8,128,256]{2,1,0:T(8,128)} %get-tuple-element.172, s32[]{:T(128)S(6)} %copy.20, bf16[256,6272]{1,0:T(8,128)(2,1)} %get-tuple-element.190, f32[6272,128]{1,0:T(8,128)} %gather_fusion, f32[6272]{0:T(1024)S(1)} %get-tuple-element.185, f32[6272]{0:T(1024)} %get-tuple-element.186, ...), kind=kOutput, calls=%fused_computation.8.clone.1 | convolution fusion | flops 414253056 | bytes 6613636 | tf_op jit(solution)/shard_map/while/body/eval_jaxpr/dot_general | solution.py:61
  72.1 0.6 dynamic_slice.11
  73.4 0.1 fusion.168
  73.5 12.6 %gather_fusion = f32[6272,128]{1,0:T(8,128)} fusion(f32[128,512]{0,1:T(8,128)S(1)} %constant_dynamic-slice_fusion.2, s32[7168]{0:T(1024)S(1)} %pad_clamp_fusion.2), kind=kCustom, calls=%fused_computation.clone.1 | custom fusion | bytes 6447616 | tf_op jit(solution)/shard_map/while/body/eval_jaxpr/jit(_take)/gather | solution.py:57
  86.1 9.6 %fusion.169 = f32[8,128,256]{2,1,0:T(8,128)} fusion(f32[8,128,256]{2,1,0:T(8,128)} %get-tuple-element.172, s32[]{:T(128)S(6)} %copy.20, bf16[256,6272]{1,0:T(8,128)(2,1)} %get-tuple-element.190, f32[6272,128]{1,0:T(8,128)} %gather_fusion, f32[6272]{0:T(1024)S(1)} %get-tuple-element.185, f32[6272]{0:T(1024)} %get-tuple-element.186, ...), kind=kOutput, calls=%fused_computation.8.clone.1 | convolution fusion | flops 414253056 | bytes 6613636 | tf_op jit(solution)/shard_map/while/body/eval_jaxpr/dot_general | solution.py:61
  95.7 0.6 dynamic_slice.11
  97.0 0.1 fusion.168
  97.1 12.6 %gather_fusion = f32[6272,128]{1,0:T(8,128)} fusion(f32[128,512]{0,1:T(8,128)S(1)} %constant_dynamic-slice_fusion.2, s32[7168]{0:T(1024)S(1)} %pad_clamp_fusion.2), kind=kCustom, calls=%fused_computation.clone.1 | custom fusion | bytes 6447616 | tf_op jit(solution)/shard_map/while/body/eval_jaxpr/jit(_take)/gather | solution.py:57
  109.7 9.6 %fusion.169 = f32[8,128,256]{2,1,0:T(8,128)} fusion(f32[8,128,256]{2,1,0:T(8,128)} %get-tuple-element.172, s32[]{:T(128)S(6)} %copy.20, bf16[256,6272]{1,0:T(8,128)(2,1)} %get-tuple-element.190, f32[6272,128]{1,0:T(8,128)} %gather_fusion, f32[6272]{0:T(1024)S(1)} %get-tuple-element.185, f32[6272]{0:T(1024)} %get-tuple-element.186, ...), kind=kOutput, calls=%fused_computation.8.clone.1 | convolution fusion | flops 414253056 | bytes 6613636 | tf_op jit(solution)/shard_map/while/body/eval_jaxpr/dot_general | solution.py:61
  119.4 0.6 dynamic_slice.11
  120.7 0.1 fusion.168
  120.8 12.6 %gather_fusion = f32[6272,128]{1,0:T(8,128)} fusion(f32[128,512]{0,1:T(8,128)S(1)} %constant_dynamic-slice_fusion.2, s32[7168]{0:T(1024)S(1)} %pad_clamp_fusion.2), kind=kCustom, calls=%fused_computation.clone.1 | custom fusion | bytes 6447616 | tf_op jit(solution)/shard_map/while/body/eval_jaxpr/jit(_take)/gather | solution.py:57
  133.4 9.6 %fusion.169 = f32[8,128,256]{2,1,0:T(8,128)} fusion(f32[8,128,256]{2,1,0:T(8,128)} %get-tuple-element.172, s32[]{:T(128)S(6)} %copy.20, bf16[256,6272]{1,0:T(8,128)(2,1)} %get-tuple-element.190, f32[6272,128]{1,0:T(8,128)} %gather_fusion, f32[6272]{0:T(1024)S(1)} %get-tuple-element.185, f32[6272]{0:T(1024)} %get-tuple-element.186, ...), kind=kOutput, calls=%fused_computation.8.clone.1 | convolution fusion | flops 414253056 | bytes 6613636 | tf_op jit(solution)/shard_map/while/body/eval_jaxpr/dot_general | solution.py:61
  143.0 0.6 dynamic_slice.11
  144.3 0.1 fusion.168
  144.4 12.6 %gather_fusion = f32[6272,128]{1,0:T(8,128)} fusion(f32[128,512]{0,1:T(8,128)S(1)} %constant_dynamic-slice_fusion.2, s32[7168]{0:T(1024)S(1)} %pad_clamp_fusion.2), kind=kCustom, calls=%fused_computation.clone.1 | custom fusion | bytes 6447616 | tf_op jit(solution)/shard_map/while/body/eval_jaxpr/jit(_take)/gather | solution.py:57
  157.0 9.6 %fusion.169 = f32[8,128,256]{2,1,0:T(8,128)} fusion(f32[8,128,256]{2,1,0:T(8,128)} %get-tuple-element.172, s32[]{:T(128)S(6)} %copy.20, bf16[256,6272]{1,0:T(8,128)(2,1)} %get-tuple-element.190, f32[6272,128]{1,0:T(8,128)} %gather_fusion, f32[6272]{0:T(1024)S(1)} %get-tuple-element.185, f32[6272]{0:T(1024)} %get-tuple-element.186, ...), kind=kOutput, calls=%fused_computation.8.clone.1 | convolution fusion | flops 414253056 | bytes 6613636 | tf_op jit(solution)/shard_map/while/body/eval_jaxpr/dot_general | solution.py:61
  166.6 0.6 dynamic_slice.11
  167.9 0.1 fusion.168
  168.0 12.6 %gather_fusion = f32[6272,128]{1,0:T(8,128)} fusion(f32[128,512]{0,1:T(8,128)S(1)} %constant_dynamic-slice_fusion.2, s32[7168]{0:T(1024)S(1)} %pad_clamp_fusion.2), kind=kCustom, calls=%fused_computation.clone.1 | custom fusion | bytes 6447616 | tf_op jit(solution)/shard_map/while/body/eval_jaxpr/jit(_take)/gather | solution.py:57
  180.6 9.6 %fusion.169 = f32[8,128,256]{2,1,0:T(8,128)} fusion(f32[8,128,256]{2,1,0:T(8,128)} %get-tuple-element.172, s32[]{:T(128)S(6)} %copy.20, bf16[256,6272]{1,0:T(8,128)(2,1)} %get-tuple-element.190, f32[6272,128]{1,0:T(8,128)} %gather_fusion, f32[6272]{0:T(1024)S(1)} %get-tuple-element.185, f32[6272]{0:T(1024)} %get-tuple-element.186, ...), kind=kOutput, calls=%fused_computation.8.clone.1 | convolution fusion | flops 414253056 | bytes 6613636 | tf_op jit(solution)/shard_map/while/body/eval_jaxpr/dot_general | solution.py:61
  190.3 0.6 dynamic_slice.11
  191.6 0.1 fusion.168
  191.7 12.6 %gather_fusion = f32[6272,128]{1,0:T(8,128)} fusion(f32[128,512]{0,1:T(8,128)S(1)} %constant_dynamic-slice_fusion.2, s32[7168]{0:T(1024)S(1)} %pad_clamp_fusion.2), kind=kCustom, calls=%fused_computation.clone.1 | custom fusion | bytes 6447616 | tf_op jit(solution)/shard_map/while/body/eval_jaxpr/jit(_take)/gather | solution.py:57
  204.3 9.6 %fusion.169 = f32[8,128,256]{2,1,0:T(8,128)} fusion(f32[8,128,256]{2,1,0:T(8,128)} %get-tuple-element.172, s32[]{:T(128)S(6)} %copy.20, bf16[256,6272]{1,0:T(8,128)(2,1)} %get-tuple-element.190, f32[6272,128]{1,0:T(8,128)} %gather_fusion, f32[6272]{0:T(1024)S(1)} %get-tuple-element.185, f32[6272]{0:T(1024)} %get-tuple-element.186, ...), kind=kOutput, calls=%fused_computation.8.clone.1 | convolution fusion | flops 414253056 | bytes 6613636 | tf_op jit(solution)/shard_map/while/body/eval_jaxpr/dot_general | solution.py:61
  214.0 0.1 fusion.120
  214.1 0.4 multiply_reduce_fusion.1
  214.5 0.4 select_multiply_fusion
  214.9 73.1 %reduce-scatter.2.cloned.1.call-done = f32[64,256]{1,0:T(8,128)} async-done(((f32[1024,256]{1,0:T(8,128)}), f32[64,256]{1,0:T(8,128)}) %reduce-scatter.2.cloned.1.call-update) | async-done | bytes 65552 | tf_op jit(solution)/shard_map/reduce_scatter | solution.py:68
  288.0 1.0 fusion.119
  289.0 62.7 %psum.21 = f32[64]{0:T(128)S(1)} all-reduce(f32[64]{0:T(128)S(1)} %broadcast_multiply_fusion), channel_id=1, replica_groups=mesh['line'=32,'bus'=16] {'line'}, use_global_device_ids=true, to_apply=%region_5.6 | all-reduce | flops 64 | bytes 512 | tf_op jit(solution)/shard_map/psum | solution.py:83
  351.7 0.8 multiply_reduce_fusion.2
  352.5 0.2 fusion.126
  352.7 28.9 %all-reduce = (f32[]{:T(128)}, f32[512]{0:T(512)S(1)}) all-reduce(f32[]{:T(128)} %get-tuple-element.96, f32[512]{0:T(512)S(1)} %bitcast.50), channel_id=1, replica_groups=mesh['line'=32,'bus'=16] {'bus'}, use_global_device_ids=true, to_apply=%region_8.9 | all-reduce | flops 513 | bytes 4104 | tf_op jit(solution)/shard_map/psum | solution.py:86
  381.6 1.2 multiply_divide_fusion
  382.8 1.3 divide_add_fusion
  (54 shorter events, 0.7 us)
Async XLA Ops:
  7.2 8.4 %copy-start = (f32[512,512]{1,0:T(8,128)S(1)}, f32[512,512]{1,0:T(8,128)}, u32[]{:S(2)}) copy-start(f32[512,512]{1,0:T(8,128)} %param.18) | copy-start | bytes 3145732
  7.2 8.3 %copy-start.3 = (f32[512]{0:T(512)S(1)}, f32[512]{0:T(512)}, u32[]{:S(2)}) copy-start(f32[512]{0:T(512)} %param.19) | copy-start | bytes 6148
  7.2 280.8 %reduce-scatter.2.cloned.1.call-start = ((), (), s32[]{:S(2)}) async-start(), calls=%async_computation.1 | async-start | bytes 1114112 | tf_op jit(solution)/shard_map/reduce_scatter | solution.py:68
  15.5 9.1 %copy-start.1 = (s32[6272]{0:T(1024)S(1)}, s32[6272]{0:T(1024)}, u32[]{:S(2)}) copy-start(s32[6272]{0:T(1024)} %param.14) | copy-start | bytes 75268
  15.5 9.1 %copy-start.6 = (f32[6272]{0:T(1024)S(1)}, f32[6272]{0:T(1024)}, u32[]{:S(2)}) copy-start(f32[6272]{0:T(1024)} %param.12) | copy-start | bytes 75268
  24.6 189.5 %copy-start.2 = (s32[8,512]{1,0:T(8,128)S(1)}, s32[8,512]{1,0:T(8,128)}, u32[]{:S(2)}) copy-start(s32[8,512]{1,0:T(8,128)} %param.17) | copy-start | bytes 49156
  24.7 189.8 %copy-start.5 = (s32[256]{0:T(256)S(1)}, s32[256]{0:T(256)}, u32[]{:S(2)}) copy-start(s32[256]{0:T(256)} %param.15) | copy-start | bytes 3076
  351.7 32.4 %copy-start.4 = (f32[64]{0:T(128)}, f32[64]{0:T(128)S(1)}, u32[]{:S(2)}) copy-start(f32[64]{0:T(128)S(1)} %psum.21) | copy-start | bytes 772
Sparse Core Ops, SparseCore 0:
  214.1 73.8 reduce-scatter.1
where the time goes:
time: 391 us
  local copies, waits for them, and re-layouts  107 us (27%)
  blocking collectives  91.6 us (23%)
  matrix products  87.2 us (22%)
  waiting for transfers between devices  73.1 us (19%)
  between operations  14.3 us (4%)
  other arithmetic  12.4 us (3%)
  loops' own time  5.64 us (1%)
    gather x8, local copies, waits for them, and re-layouts, one_block(): picked = jnp.take(rows, factor_of_bus, axis=1)  101 us
    dot_general x8, matrix products, one_block(): lax.dot_general(injections, ptdf, (((1,), (1,)), ((), ())), preferred_ele...  77.1 us
    reduce_scatter x1, waiting for transfers between devices, per_device(): lax.psum_scatter(pieces.reshape(block_rows * lax.axis_size('bus'), ptdf.s...  73.1 us
    psum x1, blocking collectives, per_device(): overload = lax.psum(share, 'line')  62.7 us
    psum x1, blocking collectives, per_device(): moved, total = lax.psum((moved_part, jnp.sum(emphasis)), 'bus')  28.9 us
    dot_general x1, matrix products, per_device(): lax.dot_general(normals(directions, shifts, 0, scenarios) + proposal_mean...  9.05 us
  transfers between devices with their start and end apart: 1, of which 1 were waited for; matrix products, arithmetic and copies ran while one was open for 0% of the time, Pallas kernels for 0%

commit v1 on v0

--- a/solution.py
+++ b/solution.py
@@ -80,7 +80,11 @@
         / SHARP
         / lines_total
     )
-    overload = lax.psum(share, "line")
+    overload = share
+    for hop in (1, 2, 4, 8, 16):
+        overload = overload + lax.ppermute(
+            overload, "line", [(dev, dev ^ hop) for dev in range(32)]
+        )
     emphasis = likelihood * overload
     moved_part = jnp.dot(emphasis, own_normals, precision=HIGH, preferred_element_type=jnp.float32)
     moved, total = lax.psum((moved_part, jnp.sum(emphasis)), "bus")

time: 391 us -> 357 us (0.913)
  the two profiles are of different devices: /device:TPU:32 before, /device:TPU:4 now
where the time goes in v1:
time: 357 us
  local copies, waits for them, and re-layouts  107 us (30%)
  matrix products  86.1 us (24%)
  waiting for transfers between devices  86.1 us (24%)
  blocking collectives  29.1 us (8%)
  starting transfers between devices  15.5 us (4%)
  between operations  14.3 us (4%)
  other arithmetic  12.9 us (4%)
  loops' own time  5.64 us (2%)
    gather x8, local copies, waits for them, and re-layouts, one_block(): picked = jnp.take(rows, factor_of_bus, axis=1)  101 us
    dot_general x8, matrix products, one_block(): lax.dot_general(injections, ptdf, (((1,), (1,)), ((), ())), preferred_ele...  76.7 us
    reduce_scatter x1, waiting for transfers between devices, per_device(): lax.psum_scatter(pieces.reshape(block_rows * lax.axis_size('bus'), ptdf.s...  74.5 us
    psum x1, blocking collectives, per_device(): moved, total = lax.psum((moved_part, jnp.sum(emphasis)), 'bus')  29.1 us
    ppermute x5, starting transfers between devices, per_device(): lax.ppermute(overload, 'line', [(dev, dev ^ hop) for dev in range(32)])  15.5 us
    ppermute x5, waiting for transfers between devices, per_device(): lax.ppermute(overload, 'line', [(dev, dev ^ hop) for dev in range(32)])  11.5 us
    dot_general x1, matrix products, per_device(): lax.dot_general(normals(directions, shifts, 0, scenarios) + proposal_mean...  9.03 us
    reduce_sum x2, other arithmetic, normals(): offset = jnp.sum(chosen[:, :, None] * shifts[None, :, :], axis=1)  7.36 us
  transfers between devices with their start and end apart: 6, of which 6 were waited for; matrix products, arithmetic and copies ran while one was open for 0% of the time, Pallas kernels for 0%

profile of v1, /device:TPU:4, one launch (start us, length us, event | category | flops | bytes accessed | tf_op | source)
XLA Modules:
  0.0 356.7 jit_solution(10230883370278333499)
XLA Ops:
  7.3 1.0 fusion.159
  8.3 0.2 fusion.115
  8.5 7.0 %multiply_reduce_fusion = s32[1024,512]{1,0:T(8,128)S(1)} fusion(s32[8,512]{1,0:T(8,128)} %param.17, s32[1024,8]{1,0:T(8,128)S(1)} %fusion.115), kind=kLoop, calls=%fused_computation.16 | loop fusion | flops 7864320 | bytes 2146304 | tf_op jit(solution)/shard_map/reduce_sum | solution.py:23
  15.6 9.0 %fusion.11 = f32[1024,512]{0,1:T(8,128)S(1)} fusion(f32[512,512]{1,0:T(8,128)S(1)} %copy-done, s32[1024,512]{1,0:T(8,128)S(1)} %multiply_reduce_fusion, f32[512]{0:T(512)S(1)} %copy-done.3, s32[512]{0:T(512)S(1)} %bitcast.46, s32[1024]{0:T(1024)S(1)} %get-tuple-element.98, s32[512]{0:T(512)S(1)} %bitcast.48, s32[1024]{0:T(1024)S(1)} %get-tuple-element.99, ...), kind=kOutput, calls=%fused_computation.20 | convolution fusion | flops 3252158464 | bytes 5287936 | tf_op jit(solution)/shard_map/dot_general | solution.py:45
  24.7 189.2 %while.10 = (s32[]{:T(128)}, f32[8,128,256]{2,1,0:T(8,128)}, f32[6272]{0:T(1024)S(1)}, f32[6272]{0:T(1024)}, s32[6272]{0:T(1024)S(1)}, /*index=5*/s32[8]{0:T(128...) while((s32[]{:T(128)}, f32[8,128,256]{2,1,0:T(8,128)}, ...), condition=%wide.region_2.3_spmd, body=%wide.region_1.2_spmd.sunk | while | flops 414316672 | bytes 13721523 | solution.py:65
  24.9 0.6 dynamic_slice.11
  26.2 12.6 %gather_fusion = f32[6272,128]{1,0:T(8,128)} fusion(f32[128,512]{0,1:T(8,128)S(1)} %constant_dynamic-slice_fusion.2, s32[7168]{0:T(1024)S(1)} %pad_clamp_fusion.2), kind=kCustom, calls=%fused_computation.clone.1 | custom fusion | bytes 6447616 | tf_op jit(solution)/shard_map/while/body/eval_jaxpr/jit(_take)/gather | solution.py:57
  38.9 9.6 %fusion.170 = f32[8,128,256]{2,1,0:T(8,128)} fusion(f32[8,128,256]{2,1,0:T(8,128)} %get-tuple-element.172, s32[]{:T(128)} %get-tuple-element.171, bf16[256,6272]{1,0:T(8,128)(2,1)} %get-tuple-element.190, f32[6272,128]{1,0:T(8,128)} %gather_fusion, f32[6272]{0:T(1024)S(1)} %get-tuple-element.185, f32[6272]{0:T(1024)} %get-tuple-element.186, ...), kind=kOutput, calls=%fused_computation.8.clone.1 | convolution fusion | flops 414253056 | bytes 6614144 | tf_op jit(solution)/shard_map/while/body/eval_jaxpr/dot_general | solution.py:61
  48.5 0.6 dynamic_slice.11
  49.9 12.6 %gather_fusion = f32[6272,128]{1,0:T(8,128)} fusion(f32[128,512]{0,1:T(8,128)S(1)} %constant_dynamic-slice_fusion.2, s32[7168]{0:T(1024)S(1)} %pad_clamp_fusion.2), kind=kCustom, calls=%fused_computation.clone.1 | custom fusion | bytes 6447616 | tf_op jit(solution)/shard_map/while/body/eval_jaxpr/jit(_take)/gather | solution.py:57
  62.5 9.6 %fusion.170 = f32[8,128,256]{2,1,0:T(8,128)} fusion(f32[8,128,256]{2,1,0:T(8,128)} %get-tuple-element.172, s32[]{:T(128)} %get-tuple-element.171, bf16[256,6272]{1,0:T(8,128)(2,1)} %get-tuple-element.190, f32[6272,128]{1,0:T(8,128)} %gather_fusion, f32[6272]{0:T(1024)S(1)} %get-tuple-element.185, f32[6272]{0:T(1024)} %get-tuple-element.186, ...), kind=kOutput, calls=%fused_computation.8.clone.1 | convolution fusion | flops 414253056 | bytes 6614144 | tf_op jit(solution)/shard_map/while/body/eval_jaxpr/dot_general | solution.py:61
  72.1 0.6 dynamic_slice.11
  73.5 12.6 %gather_fusion = f32[6272,128]{1,0:T(8,128)} fusion(f32[128,512]{0,1:T(8,128)S(1)} %constant_dynamic-slice_fusion.2, s32[7168]{0:T(1024)S(1)} %pad_clamp_fusion.2), kind=kCustom, calls=%fused_computation.clone.1 | custom fusion | bytes 6447616 | tf_op jit(solution)/shard_map/while/body/eval_jaxpr/jit(_take)/gather | solution.py:57
  86.1 9.6 %fusion.170 = f32[8,128,256]{2,1,0:T(8,128)} fusion(f32[8,128,256]{2,1,0:T(8,128)} %get-tuple-element.172, s32[]{:T(128)} %get-tuple-element.171, bf16[256,6272]{1,0:T(8,128)(2,1)} %get-tuple-element.190, f32[6272,128]{1,0:T(8,128)} %gather_fusion, f32[6272]{0:T(1024)S(1)} %get-tuple-element.185, f32[6272]{0:T(1024)} %get-tuple-element.186, ...), kind=kOutput, calls=%fused_computation.8.clone.1 | convolution fusion | flops 414253056 | bytes 6614144 | tf_op jit(solution)/shard_map/while/body/eval_jaxpr/dot_general | solution.py:61
  95.7 0.6 dynamic_slice.11
  97.1 12.6 %gather_fusion = f32[6272,128]{1,0:T(8,128)} fusion(f32[128,512]{0,1:T(8,128)S(1)} %constant_dynamic-slice_fusion.2, s32[7168]{0:T(1024)S(1)} %pad_clamp_fusion.2), kind=kCustom, calls=%fused_computation.clone.1 | custom fusion | bytes 6447616 | tf_op jit(solution)/shard_map/while/body/eval_jaxpr/jit(_take)/gather | solution.py:57
  109.8 9.6 %fusion.170 = f32[8,128,256]{2,1,0:T(8,128)} fusion(f32[8,128,256]{2,1,0:T(8,128)} %get-tuple-element.172, s32[]{:T(128)} %get-tuple-element.171, bf16[256,6272]{1,0:T(8,128)(2,1)} %get-tuple-element.190, f32[6272,128]{1,0:T(8,128)} %gather_fusion, f32[6272]{0:T(1024)S(1)} %get-tuple-element.185, f32[6272]{0:T(1024)} %get-tuple-element.186, ...), kind=kOutput, calls=%fused_computation.8.clone.1 | convolution fusion | flops 414253056 | bytes 6614144 | tf_op jit(solution)/shard_map/while/body/eval_jaxpr/dot_general | solution.py:61
  119.4 0.6 dynamic_slice.11
  120.7 12.6 %gather_fusion = f32[6272,128]{1,0:T(8,128)} fusion(f32[128,512]{0,1:T(8,128)S(1)} %constant_dynamic-slice_fusion.2, s32[7168]{0:T(1024)S(1)} %pad_clamp_fusion.2), kind=kCustom, calls=%fused_computation.clone.1 | custom fusion | bytes 6447616 | tf_op jit(solution)/shard_map/while/body/eval_jaxpr/jit(_take)/gather | solution.py:57
  133.4 9.6 %fusion.170 = f32[8,128,256]{2,1,0:T(8,128)} fusion(f32[8,128,256]{2,1,0:T(8,128)} %get-tuple-element.172, s32[]{:T(128)} %get-tuple-element.171, bf16[256,6272]{1,0:T(8,128)(2,1)} %get-tuple-element.190, f32[6272,128]{1,0:T(8,128)} %gather_fusion, f32[6272]{0:T(1024)S(1)} %get-tuple-element.185, f32[6272]{0:T(1024)} %get-tuple-element.186, ...), kind=kOutput, calls=%fused_computation.8.clone.1 | convolution fusion | flops 414253056 | bytes 6614144 | tf_op jit(solution)/shard_map/while/body/eval_jaxpr/dot_general | solution.py:61
  143.0 0.6 dynamic_slice.11
  144.4 12.6 %gather_fusion = f32[6272,128]{1,0:T(8,128)} fusion(f32[128,512]{0,1:T(8,128)S(1)} %constant_dynamic-slice_fusion.2, s32[7168]{0:T(1024)S(1)} %pad_clamp_fusion.2), kind=kCustom, calls=%fused_computation.clone.1 | custom fusion | bytes 6447616 | tf_op jit(solution)/shard_map/while/body/eval_jaxpr/jit(_take)/gather | solution.py:57
  157.0 9.6 %fusion.170 = f32[8,128,256]{2,1,0:T(8,128)} fusion(f32[8,128,256]{2,1,0:T(8,128)} %get-tuple-element.172, s32[]{:T(128)} %get-tuple-element.171, bf16[256,6272]{1,0:T(8,128)(2,1)} %get-tuple-element.190, f32[6272,128]{1,0:T(8,128)} %gather_fusion, f32[6272]{0:T(1024)S(1)} %get-tuple-element.185, f32[6272]{0:T(1024)} %get-tuple-element.186, ...), kind=kOutput, calls=%fused_computation.8.clone.1 | convolution fusion | flops 414253056 | bytes 6614144 | tf_op jit(solution)/shard_map/while/body/eval_jaxpr/dot_general | solution.py:61
  166.6 0.6 dynamic_slice.11
  168.0 12.6 %gather_fusion = f32[6272,128]{1,0:T(8,128)} fusion(f32[128,512]{0,1:T(8,128)S(1)} %constant_dynamic-slice_fusion.2, s32[7168]{0:T(1024)S(1)} %pad_clamp_fusion.2), kind=kCustom, calls=%fused_computation.clone.1 | custom fusion | bytes 6447616 | tf_op jit(solution)/shard_map/while/body/eval_jaxpr/jit(_take)/gather | solution.py:57
  180.6 9.6 %fusion.170 = f32[8,128,256]{2,1,0:T(8,128)} fusion(f32[8,128,256]{2,1,0:T(8,128)} %get-tuple-element.172, s32[]{:T(128)} %get-tuple-element.171, bf16[256,6272]{1,0:T(8,128)(2,1)} %get-tuple-element.190, f32[6272,128]{1,0:T(8,128)} %gather_fusion, f32[6272]{0:T(1024)S(1)} %get-tuple-element.185, f32[6272]{0:T(1024)} %get-tuple-element.186, ...), kind=kOutput, calls=%fused_computation.8.clone.1 | convolution fusion | flops 414253056 | bytes 6614144 | tf_op jit(solution)/shard_map/while/body/eval_jaxpr/dot_general | solution.py:61
  190.2 0.6 dynamic_slice.11
  191.6 12.6 %gather_fusion = f32[6272,128]{1,0:T(8,128)} fusion(f32[128,512]{0,1:T(8,128)S(1)} %constant_dynamic-slice_fusion.2, s32[7168]{0:T(1024)S(1)} %pad_clamp_fusion.2), kind=kCustom, calls=%fused_computation.clone.1 | custom fusion | bytes 6447616 | tf_op jit(solution)/shard_map/while/body/eval_jaxpr/jit(_take)/gather | solution.py:57
  204.2 9.6 %fusion.170 = f32[8,128,256]{2,1,0:T(8,128)} fusion(f32[8,128,256]{2,1,0:T(8,128)} %get-tuple-element.172, s32[]{:T(128)} %get-tuple-element.171, bf16[256,6272]{1,0:T(8,128)(2,1)} %get-tuple-element.190, f32[6272,128]{1,0:T(8,128)} %gather_fusion, f32[6272]{0:T(1024)S(1)} %get-tuple-element.185, f32[6272]{0:T(1024)} %get-tuple-element.186, ...), kind=kOutput, calls=%fused_computation.8.clone.1 | convolution fusion | flops 414253056 | bytes 6614144 | tf_op jit(solution)/shard_map/while/body/eval_jaxpr/dot_general | solution.py:61
  214.0 0.4 multiply_reduce_fusion.1
  214.4 74.5 %reduce-scatter.2.cloned.1.call-done = f32[64,256]{1,0:T(8,128)} async-done(((f32[1024,256]{1,0:T(8,128)}), f32[64,256]{1,0:T(8,128)}) %reduce-scatter.2.cloned.1.call-update) | async-done | bytes 65552 | tf_op jit(solution)/shard_map/reduce_scatter | solution.py:68
  288.9 1.0 fusion.119
  289.9 1.9 collective-permute-start
  291.9 1.1 collective-permute-done
  292.9 3.0 collective-permute-start.1
  295.9 2.4 collective-permute-done.1
  298.4 2.4 collective-permute-start.2
  300.8 4.5 %collective-permute-done.2 = f32[64]{0:T(128)S(1)} collective-permute-done((f32[64]{0:T(128)S(1)}, f32[64]{0:T(128)S(1)}, u32[]{:S(2)}, u32[]{:S(2)}) %collective-permute-start.2) | collective-permute-done | bytes 288 | tf_op jit(solution)/shard_map/ppermute | solution.py:85
  305.3 3.3 collective-permute-start.3
  308.6 0.4 select_multiply_fusion
  309.0 1.7 collective-permute-done.3
  310.7 4.9 %collective-permute-start.4 = (f32[64]{0:T(128)S(1)}, f32[64]{0:T(128)S(1)}, u32[]{:S(2)}, u32[]{:S(2)}) collective-permute-start(f32[64]{0:T(128)S(1)} %add.208), channel_id=1, source_target_pairs={{0,256},{16,272},{32,288},{48,304},{64,320},{80,336},{96,352},{112... | collective-permute-start | bytes 776 | tf_op jit(solution)/shard_map/ppermute | solution.py:85
  315.6 0.2 fusion.70
  315.8 1.9 collective-permute-done.4
  317.6 0.6 multiply_reduce_fusion.2
  318.4 29.1 %all-reduce = (f32[]{:T(128)}, f32[512]{0:T(512)S(1)}) all-reduce(f32[]{:T(128)} %get-tuple-element.89, f32[512]{0:T(512)S(1)} %bitcast.50), channel_id=1, replica_groups=mesh['line'=32,'bus'=16] {'bus'}, use_global_device_ids=true, to_apply=%region_7.8 | all-reduce | flops 513 | bytes 4104 | tf_op jit(solution)/shard_map/psum | solution.py:90
  347.5 1.1 multiply_divide_fusion
  348.7 1.2 divide_add_fusion
  (68 shorter events, 1.6 us)
Async XLA Ops:
  7.2 8.4 %copy-start = (f32[512,512]{1,0:T(8,128)S(1)}, f32[512,512]{1,0:T(8,128)}, u32[]{:S(2)}) copy-start(f32[512,512]{1,0:T(8,128)} %param.18) | copy-start | bytes 3145732
  7.2 8.3 %copy-start.3 = (f32[512]{0:T(512)S(1)}, f32[512]{0:T(512)}, u32[]{:S(2)}) copy-start(f32[512]{0:T(512)} %param.19) | copy-start | bytes 6148
  7.2 281.7 %reduce-scatter.2.cloned.1.call-start = ((), (), s32[]{:S(2)}) async-start(), calls=%async_computation.1 | async-start | bytes 1114112 | tf_op jit(solution)/shard_map/reduce_scatter | solution.py:68
  15.5 9.1 %copy-start.1 = (s32[6272]{0:T(1024)S(1)}, s32[6272]{0:T(1024)}, u32[]{:S(2)}) copy-start(s32[6272]{0:T(1024)} %param.14) | copy-start | bytes 75268
  15.5 9.1 %copy-start.6 = (f32[6272]{0:T(1024)S(1)}, f32[6272]{0:T(1024)}, u32[]{:S(2)}) copy-start(f32[6272]{0:T(1024)} %param.12) | copy-start | bytes 75268
  24.6 189.3 %copy-start.2 = (s32[8,512]{1,0:T(8,128)S(1)}, s32[8,512]{1,0:T(8,128)}, u32[]{:S(2)}) copy-start(s32[8,512]{1,0:T(8,128)} %param.17) | copy-start | bytes 49156
  24.6 189.7 %copy-start.5 = (s32[256]{0:T(256)S(1)}, s32[256]{0:T(256)}, u32[]{:S(2)}) copy-start(s32[256]{0:T(256)} %param.15) | copy-start | bytes 3076
  289.9 3.0 collective-permute-start
  292.9 5.4 %collective-permute-start.1 = (f32[64]{0:T(128)S(1)}, f32[64]{0:T(128)S(1)}, u32[]{:S(2)}, u32[]{:S(2)}) collective-permute-start(f32[64]{0:T(128)S(1)} %fusion.158), channel_id=1, source_target_pairs={{0,32},{16,48},{32,0},{48,16},{64,96},{80,112},{96,64},{112,80},{1... | collective-permute-start | bytes 776 | tf_op jit(solution)/shard_map/ppermute | solution.py:85
  298.4 6.9 %collective-permute-start.2 = (f32[64]{0:T(128)S(1)}, f32[64]{0:T(128)S(1)}, u32[]{:S(2)}, u32[]{:S(2)}) collective-permute-start(f32[64]{0:T(128)S(1)} %add.206), channel_id=1, source_target_pairs={{0,64},{16,80},{32,96},{48,112},{64,0},{80,16},{96,32},{112,48},{1... | collective-permute-start | bytes 776 | tf_op jit(solution)/shard_map/ppermute | solution.py:85
  305.3 5.4 %collective-permute-start.3 = (f32[64]{0:T(128)S(1)}, f32[64]{0:T(128)S(1)}, u32[]{:S(2)}, u32[]{:S(2)}) collective-permute-start(f32[64]{0:T(128)S(1)} %add.207), channel_id=1, source_target_pairs={{0,128},{16,144},{32,160},{48,176},{64,192},{80,208},{96,224},{112... | collective-permute-start | bytes 776 | tf_op jit(solution)/shard_map/ppermute | solution.py:85
  310.7 6.9 %collective-permute-start.4 = (f32[64]{0:T(128)S(1)}, f32[64]{0:T(128)S(1)}, u32[]{:S(2)}, u32[]{:S(2)}) collective-permute-start(f32[64]{0:T(128)S(1)} %add.208), channel_id=1, source_target_pairs={{0,256},{16,272},{32,288},{48,304},{64,320},{80,336},{96,352},{112... | collective-permute-start | bytes 776 | tf_op jit(solution)/shard_map/ppermute | solution.py:85
  318.2 31.6 %copy-start.4 = (f32[64]{0:T(128)}, f32[64]{0:T(128)S(1)}, u32[]{:S(2)}) copy-start(f32[64]{0:T(128)S(1)} %get-tuple-element.90) | copy-start | bytes 772
Sparse Core Ops, SparseCore 0:
  214.0 74.8 reduce-scatter.1
